TPU v7x, 128 devices: a whole 4x4x4 slice. The times are simulated.
128 devices in a mesh: dp: 8 (over x, core), fsdp: 16 (over z, y).
Axes of the slice: x: 4, y: 4, z: 4, core: 2. Of those that a mesh axis runs over, the one named last changes fastest.
Arguments:
- hidden_rows: bfloat16 [2048, 15360], P('fsdp', 'dp'), may hold values from -6 to 6
- upstream: bfloat16 [2048, 4096], P('fsdp'), may hold values from -6 to 6
- advantages: float32 [16, 4], P('fsdp'), may hold values from -4 to 4
- lengths: int32 [16, 4], P('fsdp'), may hold values from 1 to 64, 128 in all within a row
- dest_rank: int32 [256, 1], P('fsdp'), may hold values from 0 to 15; in each aligned block of 16 rows (0 to 15, 16 to 31, ...) at most 2 rows name the same one
- w_down: bfloat16 [15360, 4096], P('dp', 'fsdp'), may hold values from -0.046875 to 0.046875
Outputs:
- packed_out: bfloat16 [4096, 4096], P('fsdp', 'dp')
- packed_back: bfloat16 [4096, 15360], P('fsdp', 'dp')
- weight_grad: float32 [15360, 4096], P('dp', 'fsdp')
Inputs may be any that keep to these rules, and one draw needn't show every extreme that they name: Each generator group's 4 lengths sum to 128, the largest is 64. `dest_rank`: among the 16 blocks of one generator group, at most 2 name the same learner rank, and some learner is named 2 times.
All inputs are finite; a program needn't handle non-finite values.
Results may differ from a plain program's by a relative error of at most 0.014.
Values may be sent and summed in bfloat16 or wider, within the bound.
No kernel may reach another device: no remote copies, remote signals or barrier semaphores. Data moves between devices by JAX's collectives and lax.ppermute only.
A program may use at most 128 MiB of HBM per device.

v0:
```python
import jax
import jax.numpy as jnp
from jax import lax
from jax.sharding import PartitionSpec as P

SENDB = 2


def rounded(value):
    return lax.optimization_barrier(value.astype(jnp.bfloat16)).astype(jnp.float32)


def on_device(hidden_rows, upstream, advantages, lengths, dest_rank, w_down):
    groups = lax.axis_size("fsdp")
    src_rows = hidden_rows.shape[0]
    per_group = lengths.shape[1]
    blocks = dest_rank.shape[0]
    block_rows = src_rows // blocks
    ends_at = jnp.cumsum(lengths[0])
    starts = ends_at - lengths[0]
    position = jnp.arange(src_rows, dtype=jnp.int32)[:, None]
    member = (position >= starts[None, :]) & (position < ends_at[None, :])
    factor = advantages[0] * (src_rows / (per_group * lengths[0].astype(jnp.float32)))
    row_weight = jnp.sum(jnp.where(member, factor[None, :], jnp.float32(0.0)), axis=1)
    scaled = (row_weight[:, None] * upstream.astype(jnp.float32)).astype(jnp.bfloat16)
    w_full = lax.all_gather(w_down, "fsdp", axis=1, tiled=True)
    partial_value = lax.dot_general(
        hidden_rows, scaled, (((0,), (0,)), ((), ())), preferred_element_type=jnp.float32
    )
    weight_grad = lax.psum_scatter(
        rounded(partial_value).astype(jnp.bfloat16), "fsdp", scatter_dimension=1, tiled=True
    ).astype(jnp.float32) / (per_group * groups)
    target = dest_rank[:, 0]
    order = jnp.arange(blocks, dtype=jnp.int32)
    earlier = order[None, :] < order[:, None]
    same = target[:, None] == target[None, :]
    slot_index = jnp.sum((same & earlier).astype(jnp.int32), axis=1)
    target_slot = target * SENDB + slot_index
    one_hot = (target_slot[None, :] == jnp.arange(groups * SENDB, dtype=jnp.int32)[:, None]).astype(
        jnp.bfloat16
    )

    def place_blocks(values):
        pieces = values.reshape(blocks, block_rows, values.shape[1])
        placed = jnp.einsum(
            "ps,sbc->pbc", one_hot, pieces, preferred_element_type=jnp.float32
        ).astype(values.dtype)
        return placed.reshape(groups, SENDB * block_rows, values.shape[1])

    hidden_recv, scaled_recv = (
        lax.all_to_all(place_blocks(hidden_rows), "fsdp", split_axis=0, concat_axis=0, tiled=True),
        lax.all_to_all(place_blocks(scaled), "fsdp", split_axis=0, concat_axis=0, tiled=True),
    )
    hidden_flat = hidden_recv.reshape(-1, hidden_recv.shape[2])
    scaled_flat = scaled_recv.reshape(-1, scaled_recv.shape[2])
    forward_part = rounded(jnp.dot(hidden_flat, w_full, preferred_element_type=jnp.float32))
    packed_out = lax.psum_scatter(
        forward_part.astype(jnp.bfloat16), "dp", scatter_dimension=1, tiled=True
    )
    packed_back = lax.dot_general(
        scaled_flat, w_full, (((1,), (1,)), ((), ())), preferred_element_type=jnp.float32
    ).astype(jnp.bfloat16)
    return (packed_out, packed_back, weight_grad)


def solution(mesh):
    placed = (
        P("fsdp", "dp"),
        P("fsdp", None),
        P("fsdp", None),
        P("fsdp", None),
        P("fsdp", None),
        P("dp", "fsdp"),
    )
    return jax.shard_map(
        on_device,
        mesh=mesh,
        in_specs=placed,
        out_specs=(P("fsdp", "dp"), P("fsdp", "dp"), P("dp", "fsdp")),
        check_vma=False,
    )
```

profile of v0, /device:TPU:0, one launch (start us, length us, event | category | flops | bytes accessed | tf_op | source)
XLA Modules:
  0.0 309.7 jit_solution(16889025768865290448)
XLA Ops:
  7.2 0.7 all-gather.2.cloned.1.call-update
  8.0 0.8 reduce-window.4
  8.8 0.7 fusion.11
  9.5 0.7 fusion.10
  10.1 0.1 select_reduce_fusion
  10.2 9.4 %convert_bitcast_fusion = bf16[1920,4096]{0,1:T(8,128)(2,1)} fusion(bf16[128,1920]{1,0:T(8,128)(2,1)S(1)} %copy-done, bf16[128,4096]{1,0:T(8,128)(2,1)} %param.7, f32[128]{0:T(128)S(1)} %select_reduce_fusion), kind=kOutput, calls=%fused_computation | convolution fusion | flops 2022703104 | bytes 17269248 | tf_op jit(solution)/shard_map/dot_general | solution.py:27
  19.7 0.0 reduce-scatter.3.cloned.1.call-start
  19.7 0.6 copy-done.2
  20.3 0.2 convert_reduce_fusion
  20.5 0.5 convolution_convert_fusion.3
  21.0 0.3 copy.18
  21.3 29.7 %all_to_all.10 = bf16[16,16,1920]{2,1,0:T(8,128)(2,1)S(1)} all-to-all(bf16[16,16,1920]{2,1,0:T(8,128)(2,1)S(1)} %bitcast.32), channel_id=1, replica_groups=mesh['dp'=8,'fsdp'=16] {'fsdp'}, dimensions={0} | all-to-all | bytes 1966080 | tf_op jit(solution)/shard_map/all_to_all | solution.py:51
  51.0 85.3 %all-gather.2.cloned.1.call-done = bf16[1920,4096]{1,0:T(8,128)(2,1)} async-done(((bf16[1920,256]{1,0:T(8,128)(2,1)}), bf16[1920,4096]{1,0:T(8,128)(2,1)}) %all-gather.2.cloned.1.call-update) | async-done | bytes 15728656 | tf_op jit(solution)/shard_map/all_gather | solution.py:26
  136.4 11.5 %convolution_convert_fusion = bf16[256,4096]{1,0:T(8,128)(2,1)} fusion(bf16[256,1920]{1,0:T(8,128)(2,1)S(1)} %bitcast.34, bf16[1920,4096]{1,0:T(8,128)(2,1)} %all-gather.2.cloned.1.call-done), kind=kOutput, calls=%fused_computation.1 | convolution fusion | flops 4027580416 | bytes 18808832 | tf_op jit(solution)/shard_map/dot_general | solution.py:56
  147.9 1.5 copy-done.1
  149.4 0.3 fusion.2
  149.6 1.4 convolution_convert_fusion.1
  151.1 1.2 copy.20
  152.2 50.2 %all_to_all.11 = bf16[16,16,4096]{2,1,0:T(8,128)(2,1)S(1)} all-to-all(bf16[16,16,4096]{2,1,0:T(8,128)(2,1)S(1)} %bitcast.31), channel_id=1, replica_groups=mesh['dp'=8,'fsdp'=16] {'fsdp'}, dimensions={0} | all-to-all | bytes 4194304 | tf_op jit(solution)/shard_map/all_to_all | solution.py:52
  202.4 9.7 %convolution_convert_fusion.2 = bf16[256,1920]{1,0:T(8,128)(2,1)} fusion(bf16[256,4096]{1,0:T(8,128)(2,1)S(1)} %bitcast.33, bf16[1920,4096]{1,0:T(8,128)(2,1)} %all-gather.2.cloned.1.call-done), kind=kOutput, calls=%fused_computation.3 | convolution fusion | flops 4027023360 | bytes 18808832 | tf_op jit(solution)/shard_map/dot_general | solution.py:60
  212.0 55.4 %reduce-scatter.5.cloned.1.call-done = bf16[1920,256]{0,1:T(8,128)(2,1)} async-done(((bf16[1920,4096]{0,1:T(8,128)(2,1)}), bf16[1920,256]{0,1:T(8,128)(2,1)}) %reduce-scatter.5.cloned.1.call-update) | async-done | bytes 983056 | tf_op jit(solution)/shard_map/reduce_scatter | solution.py:30
  267.5 1.3 convert_multiply_fusion
  268.8 1.8 copy.21
  270.6 32.5 %reduce-scatter.3.cloned.1.call-done = bf16[256,512]{1,0:T(8,128)(2,1)} async-done(((bf16[256,4096]{1,0:T(8,128)(2,1)}), bf16[256,512]{1,0:T(8,128)(2,1)}) %reduce-scatter.3.cloned.1.call-update) | async-done | bytes 262160 | tf_op jit(solution)/shard_map/reduce_scatter | solution.py:57
  (9 shorter events, 0.1 us)
Async XLA Ops:
  7.2 3.1 copy-start
  7.2 129.2 %all-gather.2.cloned.1.call-start = ((), (), s32[]{:S(2)}) async-start(), calls=%async_computation.4 | async-start | bytes 16711680 | tf_op jit(solution)/shard_map/all_gather | solution.py:26
  7.9 259.6 %reduce-scatter.5.cloned.1.call-start = ((), (), s32[]{:S(2)}) async-start(), calls=%async_computation.6 | async-start | bytes 16711680 | tf_op jit(solution)/shard_map/reduce_scatter | solution.py:30
  19.6 0.7 copy-start.2
  19.7 283.5 %reduce-scatter.3.cloned.1.call-start = ((), (), s32[]{:S(2)}) async-start(), calls=%async_computation.5 | async-start | bytes 2359296 | tf_op jit(solution)/shard_map/reduce_scatter | solution.py:57
  147.8 1.5 copy-start.1
Sparse Core Ops, SparseCore 0:
  10.1 126.2 all-gather.1
  139.8 127.6 reduce-scatter.4
  270.5 32.6 reduce-scatter.2
where the time goes:
time: 310 us
  waiting for transfers between devices  174 us (56%)
  blocking collectives  79.9 us (26%)
  matrix products  32.5 us (10%)
  between operations  13.8 us (4%)
  local copies, waits for them, and re-layouts  5.33 us (2%)
  other arithmetic  4.03 us (1%)
    all_gather x1, waiting for transfers between devices, on_device(): w_full = lax.all_gather(w_down, 'fsdp', axis=1, tiled=True)  85.3 us
    reduce_scatter x1, waiting for transfers between devices, on_device(): lax.psum_scatter(rounded(partial_value).astype(jnp.bfloat16), 'fsdp', sca...  55.4 us
    all_to_all x1, blocking collectives, on_device(): lax.all_to_all(place_blocks(scaled), 'fsdp', split_axis=0, concat_axis=0,...  50.2 us
    reduce_scatter x1, waiting for transfers between devices, on_device(): lax.psum_scatter(forward_part.astype(jnp.bfloat16), 'dp', scatter_dimensi...  32.5 us
    all_to_all x1, blocking collectives, on_device(): lax.all_to_all(place_blocks(hidden_rows), 'fsdp', split_axis=0, concat_ax...  29.7 us
    dot_general x1, matrix products, on_device(): jnp.dot(hidden_flat, w_full, preferred_element_type=jnp.float32)  11.5 us
    dot_general x1, matrix products, on_device(): lax.dot_general(scaled_flat, w_full, (((1,), (1,)), ((), ())), preferred_...  9.67 us
    dot_general x1, matrix products, on_device(): lax.dot_general(hidden_rows, scaled, (((0,), (0,)), ((), ())), preferred_...  9.42 us
  transfers between devices with their start and end apart: 3, of which 3 were waited for; matrix products, arithmetic and copies ran while one was open for 13% of the time, Pallas kernels for 0%

commit v1 on v0

--- a/solution.py
+++ b/solution.py
@@ -23,7 +23,9 @@
     factor = advantages[0] * (src_rows / (per_group * lengths[0].astype(jnp.float32)))
     row_weight = jnp.sum(jnp.where(member, factor[None, :], jnp.float32(0.0)), axis=1)
     scaled = (row_weight[:, None] * upstream.astype(jnp.float32)).astype(jnp.bfloat16)
-    w_full = lax.all_gather(w_down, "fsdp", axis=1, tiled=True)
+    w_full = jnp.concatenate(
+        lax.all_to_all(jnp.stack([w_down] * lax.axis_size("fsdp")), "fsdp", 0, 0), axis=1
+    )
     partial_value = lax.dot_general(
         hidden_rows, scaled, (((0,), (0,)), ((), ())), preferred_element_type=jnp.float32
     )

time: 310 us -> 349 us (1.13)
  blocking collectives: 79.9 us -> 250 us
  waiting for transfers between devices: 174 us -> 25.5 us
  starting transfers between devices: 0.12 us -> 8.21 us
  matrix products: 32.5 us -> 37.3 us
    all_to_all x1, blocking collectives: 29.7 us -> 220 us  [on_device(): lax.all_to_all(jnp.stack([w_down] * lax.axis_size('fsdp')), 'fsdp', 0, 0)]
    all_gather x1 -> x0, waiting for transfers between devices: 85.3 us -> none  [on_device(): w_full = lax.all_gather(w_down, 'fsdp', axis=1, tiled=True)]
    reduce_scatter x1, waiting for transfers between devices: 55.4 us -> 0.01 us  [on_device(): lax.psum_scatter(rounded(partial_value).astype(jnp.bfloat16), 'fsdp', sca...]
    reduce_scatter x1, waiting for transfers between devices: 32.5 us -> 0.01 us  [on_device(): lax.psum_scatter(forward_part.astype(jnp.bfloat16), 'dp', scatter_dimensi...]
    all_to_all x0 -> x1, waiting for transfers between devices: none -> 25.5 us  [on_device(): lax.all_to_all(place_blocks(hidden_rows), 'fsdp', split_axis=0, concat_ax...]
    all_to_all x1, blocking collectives: 50.2 us -> 30.4 us  [on_device(): lax.all_to_all(place_blocks(scaled), 'fsdp', split_axis=0, concat_axis=0,...]
    all_to_all x0 -> x1, starting transfers between devices: none -> 8.13 us  [on_device(): lax.all_to_all(place_blocks(hidden_rows), 'fsdp', split_axis=0, concat_ax...]
    dot_general x1, matrix products: 11.5 us -> 16.8 us  [on_device(): jnp.dot(hidden_flat, w_full, preferred_element_type=jnp.float32)]
  transfers between devices with their start and end apart: 3 -> 3, of which waited for: 3 -> 1; matrix products, arithmetic and copies ran while one was open for 13% -> 10% of each run, Pallas kernels for 0% -> 0%
where the time goes in v1:
time: 349 us; the launch traced here: 348 us
  blocking collectives  250 us (72%)
  matrix products  37.3 us (11%)
  waiting for transfers between devices  25.5 us (7%)
  between operations  14.1 us (4%)
  local copies, waits for them, and re-layouts  8.77 us (3%)
  starting transfers between devices  8.21 us (2%)
  other arithmetic  4.13 us (1%)
    all_to_all x1, blocking collectives, on_device(): lax.all_to_all(jnp.stack([w_down] * lax.axis_size('fsdp')), 'fsdp', 0, 0)  220 us
    all_to_all x1, blocking collectives, on_device(): lax.all_to_all(place_blocks(scaled), 'fsdp', split_axis=0, concat_axis=0,...  30.4 us
    all_to_all x1, waiting for transfers between devices, on_device(): lax.all_to_all(place_blocks(hidden_rows), 'fsdp', split_axis=0, concat_ax...  25.5 us
    dot_general x1, matrix products, on_device(): jnp.dot(hidden_flat, w_full, preferred_element_type=jnp.float32)  16.8 us
    dot_general x1, matrix products, on_device(): lax.dot_general(hidden_rows, scaled, (((0,), (0,)), ((), ())), preferred_...  9.53 us
    dot_general x1, matrix products, on_device(): lax.dot_general(scaled_flat, w_full, (((1,), (1,)), ((), ())), preferred_...  9.06 us
    all_to_all x1, starting transfers between devices, on_device(): lax.all_to_all(place_blocks(hidden_rows), 'fsdp', split_axis=0, concat_ax...  8.13 us
  transfers between devices with their start and end apart: 3, of which 1 were waited for; matrix products, arithmetic and copies ran while one was open for 10% of the time, Pallas kernels for 0%

profile of v1, /device:TPU:0, one launch (start us, length us, event | category | flops | bytes accessed | tf_op | source)
XLA Modules:
  0.0 348.5 jit_solution(14597172058874316812)
XLA Ops:
  7.2 0.7 fusion.11
  8.0 0.8 reduce-window.4
  8.8 0.7 fusion.10
  9.4 0.1 select_reduce_fusion
  9.5 9.5 %convert_bitcast_fusion = bf16[1920,4096]{0,1:T(8,128)(2,1)} fusion(bf16[128,1920]{1,0:T(8,128)(2,1)S(1)} %copy-done, bf16[128,4096]{1,0:T(8,128)(2,1)} %param.7, f32[128]{0:T(128)S(1)} %select_reduce_fusion), kind=kOutput, calls=%fused_computation | convolution fusion | flops 2022703104 | bytes 17269248 | tf_op jit(solution)/shard_map/dot_general | solution.py:29
  19.1 0.6 copy-done.4
  19.7 0.2 convert_reduce_fusion
  19.9 0.5 convolution_convert_fusion.3
  20.5 1.2 copy.19
  21.7 8.1 %all-to-all-start = ((bf16[16,16,1920]{2,1,0:T(8,128)(2,1)}), bf16[16,16,1920]{2,1,0:T(8,128)(2,1)S(1)}, u32[]{:S(2)}, u32[]{:S(2)}) async-start(bf16[16,16,1920]{2,1,0:T(8,128)(2,1)} %bitcast.3), calls=%async_computation | async-start | bytes 1966080 | tf_op jit(solution)/shard_map/all_to_all | solution.py:53
  29.8 0.0 reduce-scatter.3.cloned.1.call-start
  29.9 0.7 copy.20
  30.6 25.5 %all-to-all-done = bf16[16,16,1920]{2,1,0:T(8,128)(2,1)S(1)} async-done(((bf16[16,16,1920]{2,1,0:T(8,128)(2,1)}), bf16[16,16,1920]{2,1,0:T(8,128)(2,1)S(1)}, u32[]{:S(2)}, u32[]{:S(2)}) %all-to-all-start) | async-done | bytes 983072 | tf_op jit(solution)/shard_map/all_to_all | solution.py:53
  56.1 2.0 stack.2
  58.1 220.0 %all_to_all.15 = bf16[16,1920,256]{1,2,0:T(8,128)(2,1)} all-to-all(bf16[16,1920,256]{1,2,0:T(8,128)(2,1)S(1)} %stack.2), channel_id=1, replica_groups=mesh['dp'=8,'fsdp'=16] {'fsdp'}, dimensions={0} | all-to-all | bytes 31457280 | tf_op jit(solution)/shard_map/all_to_all | solution.py:27
  278.1 16.8 %convolution_convert_fusion = bf16[256,4096]{1,0:T(8,128)(2,1)} fusion(bf16[256,1920]{1,0:T(8,128)(2,1)S(1)} %bitcast.38, bf16[1920,4096]{0,1:T(8,128)(2,1)} %bitcast.34), kind=kOutput, calls=%fused_computation.1 | convolution fusion | flops 4027580416 | bytes 18808832 | tf_op jit(solution)/shard_map/dot_general | solution.py:58
  295.0 1.2 copy-done.2
  296.1 0.3 fusion.2
  296.4 1.4 convolution_convert_fusion.1
  297.8 1.2 copy.22
  299.0 30.4 %all_to_all.16 = bf16[16,16,4096]{2,1,0:T(8,128)(2,1)S(1)} all-to-all(bf16[16,16,4096]{2,1,0:T(8,128)(2,1)S(1)} %bitcast.36), channel_id=1, replica_groups=mesh['dp'=8,'fsdp'=16] {'fsdp'}, dimensions={0} | all-to-all | bytes 4194304 | tf_op jit(solution)/shard_map/all_to_all | solution.py:54
  329.4 9.1 %convolution_convert_fusion.2 = bf16[256,1920]{1,0:T(8,128)(2,1)} fusion(bf16[256,4096]{1,0:T(8,128)(2,1)S(1)} %bitcast.37, bf16[1920,4096]{0,1:T(8,128)(2,1)} %bitcast.35), kind=kOutput, calls=%fused_computation.3 | convolution fusion | flops 4027023360 | bytes 18808832 | tf_op jit(solution)/shard_map/dot_general | solution.py:62
  338.4 1.4 convert_multiply_fusion
  339.8 1.8 copy.23
  (14 shorter events, 0.1 us)
Async XLA Ops:
  7.2 2.4 copy-start
  7.2 331.3 %reduce-scatter.5.cloned.1.call-start = ((), (), s32[]{:S(2)}) async-start(), calls=%async_computation.6 | async-start | bytes 16711680 | tf_op jit(solution)/shard_map/reduce_scatter | solution.py:32
  19.1 0.7 copy-start.4
  20.4 9.4 %copy-start.3 = (bf16[1920,256]{1,0:T(8,128)(2,1)S(1)}, bf16[1920,256]{1,0:T(8,128)(2,1)}, u32[]{:S(2)}) copy-start(bf16[1920,256]{1,0:T(8,128)(2,1)} %param.11) | copy-start | bytes 2949124
  21.7 34.4 %all-to-all-start = ((bf16[16,16,1920]{2,1,0:T(8,128)(2,1)}), bf16[16,16,1920]{2,1,0:T(8,128)(2,1)S(1)}, u32[]{:S(2)}, u32[]{:S(2)}) async-start(bf16[16,16,1920]{2,1,0:T(8,128)(2,1)} %bitcast.3), calls=%async_computation | async-start | bytes 1966080 | tf_op jit(solution)/shard_map/all_to_all | solution.py:53
  29.8 311.8 %reduce-scatter.3.cloned.1.call-start = ((), (), s32[]{:S(2)}) async-start(), calls=%async_computation.5 | async-start | bytes 2359296 | tf_op jit(solution)/shard_map/reduce_scatter | solution.py:59
  294.9 1.2 copy-start.2
  338.4 3.2 copy-start.1
Sparse Core Ops, SparseCore 0:
  19.2 285.9 reduce-scatter.4
  308.1 33.1 reduce-scatter.2
